TPU v7x, 128 devices: a whole 4x4x4 slice. The times are simulated.
128 devices in a mesh: dp: 8 (over z_lo, x), seq: 16 (over z_hi, y, core).
Axes of the slice: x: 4, y: 4, z: 4 (z_hi: 2, z_lo: 2; z = z_hi * 2 + z_lo), core: 2. Of those that a mesh axis runs over, the one named last changes fastest.
Arguments:
- series: bfloat16 [8, 8192, 128], P('dp', 'seq'), may hold values from -6 to 6
- cotangent: bfloat16 [8, 8192, 128], P('dp', 'seq'), may hold values from -6 to 6
- w_in: bfloat16 [128, 384], replicated, may hold values from -0.5 to 0.5
- w_out: bfloat16 [128, 128], replicated, may hold values from -0.5 to 0.5
- taps: float32 [3, 384], replicated, may hold values from -3 to 3
- skip_one: float32 [128], replicated, may hold values from 0.5 to 1.5
- skip_two: float32 [128], replicated, may hold values from 0.5 to 1.5
- filter_one: float32 [8, 8192], P(None, 'seq'), may hold values from -0.0625 to 0.0625
- filter_two: float32 [8, 8192], P(None, 'seq'), may hold values from -0.0625 to 0.0625
Outputs:
- output: bfloat16 [8, 8192, 128], P('dp', 'seq')
- d_series: bfloat16 [8, 8192, 128], P('dp', 'seq')
- grad_w_in: float32 [128, 384], replicated
- grad_w_out: float32 [128, 128], replicated
- grad_taps: float32 [3, 384], replicated
- grad_skip_one: float32 [128], replicated
- grad_skip_two: float32 [128], replicated
- grad_filter_one: float32 [8, 8192], P(None, 'seq')
- grad_filter_two: float32 [8, 8192], P(None, 'seq')
All inputs are finite; a program needn't handle non-finite values.
Results may differ from a plain program's by a relative error of at most 0.015.
Values may be sent and summed in bfloat16 or wider, within the bound.
A program may use at most 128 MiB of HBM per device.

v0:
```python
import math
import numpy as np
import jax
import jax.numpy as jnp
from jax import lax
from jax.sharding import PartitionSpec as P

HIGHEST = lax.Precision.HIGHEST
LANES = 128


def dft_tables(length):
    size = 2 * length
    rows = size // LANES
    half = length // LANES
    k1 = np.arange(rows)
    f1 = np.exp(-2j * np.pi * (np.outer(k1, np.arange(half)) % rows) / rows)
    turn = np.exp(-2j * np.pi * np.outer(k1, np.arange(LANES)) / size)
    f2 = np.exp(-2j * np.pi * (np.outer(np.arange(LANES), np.arange(LANES)) % LANES) / LANES)
    fwd1 = np.concatenate([f1.real, f1.imag], axis=0)
    fwd2 = np.block([[f2.real, f2.imag], [-f2.imag, f2.real]])
    inv2 = np.block([[f2.real, -f2.imag], [f2.imag, f2.real]])
    inv1 = np.concatenate([f1.real.T, f1.imag.T], axis=1) / size
    as32 = lambda a: jnp.asarray(np.asarray(a, np.float32))
    return {
        "rows": rows,
        "fwd1": as32(fwd1),
        "fwd2": as32(fwd2),
        "inv1": as32(inv1),
        "inv2": as32(inv2),
        "turn_r": as32(turn.real)[:, None, :],
        "turn_i": as32(turn.imag)[:, None, :],
    }


def spectrum(x, tab):
    rows = tab["rows"]
    a = jnp.einsum("kn,ncm->kcm", tab["fwd1"], x, precision=HIGHEST)
    ar, ai = (a[:rows], a[rows:])
    tr, ti = (tab["turn_r"], tab["turn_i"])
    cat = jnp.concatenate([ar * tr - ai * ti, ar * ti + ai * tr], axis=-1)
    return jnp.einsum("kcm,mj->kcj", cat, tab["fwd2"], precision=HIGHEST)


def signal(s, tab):
    b = jnp.einsum("kcj,jm->kcm", s, tab["inv2"], precision=HIGHEST)
    br, bi = (b[..., :LANES], b[..., LANES:])
    tr, ti = (tab["turn_r"], tab["turn_i"])
    stacked = jnp.concatenate([br * tr + bi * ti, bi * tr - br * ti], axis=0)
    return jnp.einsum("nk,kcm->ncm", tab["inv1"], stacked, precision=HIGHEST)


def cmul(a, b, conj=False):
    ar, ai = (a[..., :LANES], a[..., LANES:])
    br, bi = (b[..., :LANES], b[..., LANES:])
    if conj:
        bi = -bi
    return jnp.concatenate([ar * br - ai * bi, ar * bi + ai * br], axis=-1)


def fold(x):
    c, length = x.shape
    return jnp.swapaxes(x.reshape(c, length // LANES, LANES), 0, 1)


def unfold(x):
    half, c, lanes = x.shape
    return jnp.swapaxes(x, 0, 1).reshape(c, half * lanes)


def shards(series, cotangent, w_in, w_out, taps, skip_one, skip_two, filter_one, filter_two):
    _, block, width = series.shape
    seq_n = lax.axis_size("seq")
    dp_n = lax.axis_size("dp")
    length = block * seq_n
    half = length // LANES
    me = lax.axis_index("seq")
    per = width // seq_n
    filters = filter_one.shape[0]
    group_width = width // filters
    per_group = group_width // per
    group = me // per_group
    grad_scale = 1.0 / math.sqrt(dp_n * series.shape[0] * length)
    tab = dft_tables(length)
    rows_sent = jnp.repeat(
        jnp.swapaxes(jnp.stack([filter_one, filter_two]), 0, 1), per_group, axis=0
    )
    rows_got = lax.all_to_all(rows_sent, "seq", 0, 0, tiled=True)
    h_rows = jnp.swapaxes(rows_got, 0, 1).reshape(2, length)
    taps_sel = lax.dynamic_index_in_dim(
        taps.reshape(3, 3, seq_n, per), me, axis=2, keepdims=False
    ).reshape(3, 3 * per)
    skip1 = lax.dynamic_index_in_dim(skip_one.reshape(seq_n, per), me, axis=0, keepdims=False)
    skip2 = lax.dynamic_index_in_dim(skip_two.reshape(seq_n, per), me, axis=0, keepdims=False)
    skip1 = skip1[None, :, None]
    skip2 = skip2[None, :, None]
    proj_blk = jnp.einsum("td,dc->ct", series[0], w_in, preferred_element_type=jnp.float32)
    proj_blk = lax.all_to_all(proj_blk.reshape(3, seq_n, per, block), "seq", 1, 1, tiled=True)
    proj = jnp.swapaxes(proj_blk, 1, 2).reshape(3 * per, length)
    prev1 = jnp.pad(proj, ((0, 0), (1, 0)))[:, :length]
    prev2 = jnp.pad(proj, ((0, 0), (2, 0)))[:, :length]
    conv = taps_sel[0][:, None] * proj + taps_sel[1][:, None] * prev1 + taps_sel[2][:, None] * prev2
    conv_f = fold(conv)
    value = conv_f[:, :per]
    gate_one = conv_f[:, per : 2 * per]
    gate_two = conv_f[:, 2 * per :]
    h_spec = spectrum(fold(h_rows), tab)
    h_one = h_spec[:, 0:1]
    h_two = h_spec[:, 1:2]
    v_spec = spectrum(value, tab)
    y_one = signal(cmul(v_spec, h_one), tab) + skip1 * value
    gated_mid = gate_one * y_one
    m_spec = spectrum(gated_mid, tab)
    y_two = signal(cmul(m_spec, h_two), tab) + skip2 * gated_mid
    product = (gate_two * y_two).astype(jnp.bfloat16)
    dprod_blk = jnp.einsum("td,cd->ct", cotangent[0], w_out, preferred_element_type=jnp.float32)
    dprod_blk = lax.all_to_all(dprod_blk.reshape(seq_n, per, block), "seq", 0, 0, tiled=True)
    d_product = jnp.swapaxes(dprod_blk.reshape(seq_n, per, block // LANES, LANES), 1, 2).reshape(
        half, per, LANES
    )
    grad_two = d_product * gate_two
    d_gate_two = d_product * y_two
    g2_spec = spectrum(grad_two, tab)
    d_mid = signal(cmul(g2_spec, h_two, conj=True), tab) + skip2 * grad_two
    grad_one = d_mid * gate_one
    d_gate_one = d_mid * y_one
    g1_spec = spectrum(grad_one, tab)
    d_value = signal(cmul(g1_spec, h_one, conj=True), tab) + skip1 * grad_one
    corr = jnp.concatenate(
        [
            jnp.sum(cmul(g1_spec, v_spec, conj=True), axis=1, keepdims=True),
            jnp.sum(cmul(g2_spec, m_spec, conj=True), axis=1, keepdims=True),
        ],
        axis=1,
    )
    filt_grad = unfold(signal(corr, tab))
    d_conv = unfold(jnp.concatenate([d_value, d_gate_one, d_gate_two], axis=1))
    next1 = jnp.pad(d_conv, ((0, 0), (0, 1)))[:, 1:]
    next2 = jnp.pad(d_conv, ((0, 0), (0, 2)))[:, 2:]
    d_proj = (
        taps_sel[0][:, None] * d_conv + taps_sel[1][:, None] * next1 + taps_sel[2][:, None] * next2
    ).astype(jnp.bfloat16)
    local_taps = jnp.stack(
        [
            jnp.sum(d_conv * proj, axis=1),
            jnp.sum(d_conv * prev1, axis=1),
            jnp.sum(d_conv * prev2, axis=1),
        ]
    )
    local_skip1 = jnp.sum(grad_one * value, axis=(0, 2))
    local_skip2 = jnp.sum(grad_two * gated_mid, axis=(0, 2))
    prod_blocks = product.reshape(seq_n, half // seq_n, per, LANES)
    prod_blocks = lax.all_to_all(prod_blocks, "seq", 0, 0, tiled=True)
    output = jnp.einsum(
        "jnim,jid->nmd",
        prod_blocks,
        w_out.reshape(seq_n, per, width),
        preferred_element_type=jnp.float32,
    ).astype(jnp.bfloat16)
    output = output.reshape(1, block, width)
    dp_blocks = d_proj.reshape(3, per, seq_n, block)
    dp_blocks = lax.all_to_all(dp_blocks, "seq", 2, 2, tiled=True)
    d_series = jnp.einsum(
        "pijt,dpji->td",
        dp_blocks,
        w_in.reshape(width, 3, seq_n, per),
        preferred_element_type=jnp.float32,
    ).astype(jnp.bfloat16)
    d_series = d_series.reshape(1, block, width)
    fg_blocks = lax.all_to_all(filt_grad.reshape(2, seq_n, block), "seq", 1, 1, tiled=True)
    fg_blocks = jnp.sum(fg_blocks.reshape(2, filters, per_group, block), axis=2)
    prod_rows = jnp.transpose(prod_blocks, (1, 3, 0, 2)).reshape(block, width)
    dp_rows = jnp.transpose(dp_blocks, (3, 0, 2, 1)).reshape(block, 3 * width)
    local_w_in = jnp.einsum("td,tc->dc", series[0], dp_rows, preferred_element_type=jnp.float32)
    local_w_out = jnp.einsum(
        "tc,td->cd", prod_rows, cotangent[0], preferred_element_type=jnp.float32
    )
    small = jnp.concatenate(
        [
            local_taps.reshape(3, 3, 1, per),
            jnp.stack([local_skip1, local_skip2, jnp.zeros_like(local_skip1)]).reshape(
                3, 1, 1, per
            ),
        ],
        axis=1,
    )
    small_full = jnp.zeros((3, 4, seq_n, per), jnp.float32)
    small_full = lax.dynamic_update_slice(small_full, small, (0, 0, me, 0))
    grad_w_in, grad_w_out, small_full = lax.psum(
        (local_w_in, local_w_out, small_full), ("dp", "seq")
    )
    fg_blocks = lax.psum(fg_blocks, "dp")
    small_full = small_full.reshape(3, 4, width)
    grad_taps = small_full[:, :3].reshape(3, 3 * width)
    grad_skip_one = small_full[0, 3]
    grad_skip_two = small_full[1, 3]
    return (
        output,
        d_series,
        grad_scale * grad_w_in,
        grad_scale * grad_w_out,
        grad_scale * grad_taps,
        grad_scale * grad_skip_one,
        grad_scale * grad_skip_two,
        grad_scale * fg_blocks[0],
        grad_scale * fg_blocks[1],
    )


def solution(mesh):
    in_specs = (
        P("dp", "seq", None),
        P("dp", "seq", None),
        P(),
        P(),
        P(),
        P(),
        P(),
        P(None, "seq"),
        P(None, "seq"),
    )
    out_specs = (
        P("dp", "seq", None),
        P("dp", "seq", None),
        P(),
        P(),
        P(),
        P(),
        P(),
        P(None, "seq"),
        P(None, "seq"),
    )
    return jax.shard_map(shards, mesh=mesh, in_specs=in_specs, out_specs=out_specs, check_vma=False)
```

profile of v0, /device:TPU:1, one launch (start us, length us, event | category | flops | bytes accessed | tf_op | source)
XLA Modules:
  0.0 364.3 jit_solution(12172871343249868817)
XLA Ops:
  8.6 9.4 %all-to-all-start.1 = ((f32[16,2,512]{2,1,0:T(2,128)}), f32[16,2,512]{2,1,0:T(2,128)S(1)}, u32[]{:S(2)}, u32[]{:S(2)}) async-start(f32[16,2,512]{2,1,0:T(2,128)} %bitcast.12), calls=%async_computation.1 | async-start | bytes 131072 | tf_op jit(solution)/shard_map/all_to_all | solution.py:88
  20.6 1.2 fusion.68
  22.7 2.7 all-to-all-done.1
  25.4 4.6 %all-to-all-start.3 = ((f32[16,8,512]{2,1,0:T(8,128)}), f32[16,8,512]{2,1,0:T(8,128)S(1)}, u32[]{:S(2)}, u32[]{:S(2)}) async-start(f32[16,8,512]{2,1,0:T(8,128)} %fusion.70), calls=%async_computation.3 | async-start | bytes 524288 | tf_op jit(solution)/shard_map/all_to_all | solution.py:117
  31.8 6.9 %all-to-all-done.3 = f32[16,8,512]{2,1,0:T(8,128)S(1)} async-done(((f32[16,8,512]{2,1,0:T(8,128)}), f32[16,8,512]{2,1,0:T(8,128)S(1)}, u32[]{:S(2)}, u32[]{:S(2)}) %all-to-all-start.3) | async-done | bytes 262176 | tf_op jit(solution)/shard_map/all_to_all | solution.py:117
  38.7 4.2 %all-to-all-start = ((f32[3,16,8,512]{3,2,0,1:T(8,128)}), f32[3,16,8,512]{3,2,0,1:T(8,128)S(1)}, u32[]{:S(2)}, u32[]{:S(2)}) async-start(f32[3,16,8,512]{3,2,0,1:T(8,128)} %fusion.68), calls=%async_computation | async-start | bytes 1572864 | tf_op jit(solution)/shard_map/all_to_all | solution.py:98
  43.6 13.9 %all-to-all-done = f32[3,16,8,512]{3,2,0,1:T(8,128)S(1)} async-done(((f32[3,16,8,512]{3,2,0,1:T(8,128)}), f32[3,16,8,512]{3,2,0,1:T(8,128)S(1)}, u32[]{:S(2)}, u32[]{:S(2)}) %all-to-all-start) | async-done | bytes 786464 | tf_op jit(solution)/shard_map/all_to_all | solution.py:98
  59.1 1.0 fusion.64
  60.2 1.0 fusion.102
  61.3 1.9 fusion.25
  64.1 1.1 fusion.29
  66.1 1.1 convolution_add_fusion.1
  67.3 1.0 fusion.101
  68.5 1.9 fusion.3
  70.4 2.0 fusion.36
  72.9 1.1 fusion.7
  74.0 1.1 fusion.40
  75.4 1.1 convolution_add_fusion.3
  76.5 1.0 fusion.100
  77.7 1.9 fusion.14
  79.8 1.1 fusion.18
  81.1 1.1 convolution_add_fusion
  82.2 1.2 multiply_reduce_fusion.3
  86.7 4.0 %all-to-all-start.5 = ((f32[2,16,512]{2,0,1:T(2,128)}), f32[2,16,512]{2,0,1:T(2,128)S(1)}, u32[]{:S(2)}, u32[]{:S(2)}) async-start(f32[2,16,512]{2,0,1:T(2,128)} %copy.198), calls=%async_computation.5 | async-start | bytes 131072 | tf_op jit(solution)/shard_map/all_to_all | solution.py:170
  91.5 67.0 %psum.30 = f32[3,4,128]{2,1,0:T(4,128)S(1)} all-reduce(f32[3,4,128]{2,1,0:T(4,128)S(1)} %reshape.136), channel_id=1, replica_groups=mesh['dp'=8,'seq'=16] {'dp','seq'}, use_global_device_ids=true, to_apply=%region_7.8 | all-reduce | flops 1536 | bytes 12288 | tf_op jit(solution)/shard_map/psum | solution.py:189
  160.2 1.0 copy.188
  161.9 4.3 %all-to-all-start.2 = ((bf16[16,4,8,128]{3,2,1,0:T(8,128)(2,1)}), bf16[16,4,8,128]{3,2,1,0:T(8,128)(2,1)S(1)}, u32[]{:S(2)}, u32[]{:S(2)}) async-start(bf16[16,4,8,128]{3,2,1,0:T(8,128)(2,1)} %copy.177), calls=%async_computation.2 | async-start | bytes 262144 | tf_op jit(solution)/shard_map/all_to_all | solution.py:153
  166.3 25.2 %psum.31 = f32[2,8,512]{2,0,1:T(2,128)S(1)} all-reduce(f32[2,8,512]{2,0,1:T(2,128)S(1)} %bitcast_reduce_fusion), channel_id=1, replica_groups=mesh['dp'=8,'seq'=16] {'dp'}, use_global_device_ids=true, to_apply=%region_11.12 | all-reduce | flops 8192 | bytes 65536 | tf_op jit(solution)/shard_map/psum | solution.py:192
  192.7 14.6 %all-to-all-start.4 = ((bf16[3,8,16,512]{3,1,0,2:T(8,128)(2,1)}), bf16[3,8,16,512]{3,1,0,2:T(8,128)(2,1)S(1)}, u32[]{:S(2)}, u32[]{:S(2)}) async-start(bf16[3,8,16,512]{3,1,0,2:T(8,128)(2,1)} %copy.188), calls=%async_computation.4 | async-start | bytes 786432 | tf_op jit(solution)/shard_map/all_to_all | solution.py:162
  209.0 8.0 %all-to-all-done.4 = bf16[3,8,16,512]{3,1,0,2:T(8,128)(2,1)S(1)} async-done(((bf16[3,8,16,512]{3,1,0,2:T(8,128)(2,1)}), bf16[3,8,16,512]{3,1,0,2:T(8,128)(2,1)S(1)}, u32[]{:S(2)}, u32[]{:S(2)}) %all-to-all-start.4) | async-done | bytes 393248 | tf_op jit(solution)/shard_map/all_to_all | solution.py:162
  218.1 1.0 fusion.2
  219.0 136.0 %all-reduce.7.cloned.1.call-done = (f32[128,384]{0,1:T(8,128)}, f32[128,128]{1,0:T(8,128)}) async-done(((f32[128,384]{0,1:T(8,128)}, f32[128,128]{1,0:T(8,128)}), (f32[128,384]{0,1:T(8,128)}, f32[128,128]{1,0:T(8,128)})) %all-reduce.7.cloned.1.call-update) | async-done | bytes 262160 | tf_op jit(solution)/shard_map/psum | solution.py:189
  (105 shorter events, 25.0 us)
Async XLA Ops:
  7.2 13.4 %copy-start = (bf16[1,512,128]{2,1,0:T(8,128)(2,1)S(1)}, bf16[1,512,128]{2,1,0:T(8,128)(2,1)}, u32[]{:S(2)}) copy-start(bf16[1,512,128]{2,1,0:T(8,128)(2,1)} %param.15) | copy-start | bytes 393220
  8.6 10.5 %copy-start.8 = (bf16[128,384]{1,0:T(8,128)(2,1)S(1)}, bf16[128,384]{1,0:T(8,128)(2,1)}, u32[]{:S(2)}) copy-start(bf16[128,384]{1,0:T(8,128)(2,1)} %param.17) | copy-start | bytes 294916
  8.6 16.8 %all-to-all-start.1 = ((f32[16,2,512]{2,1,0:T(2,128)}), f32[16,2,512]{2,1,0:T(2,128)S(1)}, u32[]{:S(2)}, u32[]{:S(2)}) async-start(f32[16,2,512]{2,1,0:T(2,128)} %bitcast.12), calls=%async_computation.1 | async-start | bytes 131072 | tf_op jit(solution)/shard_map/all_to_all | solution.py:88
  18.1 0.7 copy-start.11
  19.2 0.7 copy-start.12
  19.8 0.7 copy-start.13
  20.6 1.2 copy-start.7
  20.6 1.2 copy-start.10
  25.4 13.3 %all-to-all-start.3 = ((f32[16,8,512]{2,1,0:T(8,128)}), f32[16,8,512]{2,1,0:T(8,128)S(1)}, u32[]{:S(2)}, u32[]{:S(2)}) async-start(f32[16,8,512]{2,1,0:T(8,128)} %fusion.70), calls=%async_computation.3 | async-start | bytes 524288 | tf_op jit(solution)/shard_map/all_to_all | solution.py:117
  30.0 0.8 copy-start.6
  30.8 0.8 copy-start.3
  30.8 0.9 copy-start.4
  31.7 11.1 %copy-start.2 = (f32[256,256,1]{1,0,2:T(8,128)S(1)}, f32[256,256,1]{1,0,2:T(8,128)}, u32[]{:S(2)}) copy-start(f32[256,256,1]{1,0,2:T(8,128)} %constant.59) | copy-start | bytes 786436
  38.7 18.8 %all-to-all-start = ((f32[3,16,8,512]{3,2,0,1:T(8,128)}), f32[3,16,8,512]{3,2,0,1:T(8,128)S(1)}, u32[]{:S(2)}, u32[]{:S(2)}) async-start(f32[3,16,8,512]{3,2,0,1:T(8,128)} %fusion.68), calls=%async_computation | async-start | bytes 1572864 | tf_op jit(solution)/shard_map/all_to_all | solution.py:98
  63.2 1.0 copy-start.1
  65.3 0.8 copy-start.5
  86.7 75.3 %all-to-all-start.5 = ((f32[2,16,512]{2,0,1:T(2,128)}), f32[2,16,512]{2,0,1:T(2,128)S(1)}, u32[]{:S(2)}, u32[]{:S(2)}) async-start(f32[2,16,512]{2,0,1:T(2,128)} %copy.198), calls=%async_computation.5 | async-start | bytes 131072 | tf_op jit(solution)/shard_map/all_to_all | solution.py:170
  161.9 30.8 %all-to-all-start.2 = ((bf16[16,4,8,128]{3,2,1,0:T(8,128)(2,1)}), bf16[16,4,8,128]{3,2,1,0:T(8,128)(2,1)S(1)}, u32[]{:S(2)}, u32[]{:S(2)}) async-start(bf16[16,4,8,128]{3,2,1,0:T(8,128)(2,1)} %copy.177), calls=%async_computation.2 | async-start | bytes 262144 | tf_op jit(solution)/shard_map/all_to_all | solution.py:153
  192.7 24.4 %all-to-all-start.4 = ((bf16[3,8,16,512]{3,1,0,2:T(8,128)(2,1)}), bf16[3,8,16,512]{3,1,0,2:T(8,128)(2,1)S(1)}, u32[]{:S(2)}, u32[]{:S(2)}) async-start(bf16[3,8,16,512]{3,1,0,2:T(8,128)(2,1)} %copy.188), calls=%async_computation.4 | async-start | bytes 786432 | tf_op jit(solution)/shard_map/all_to_all | solution.py:162
  207.3 147.7 %all-reduce.7.cloned.1.call-start = ((), (), s32[]{:S(2)}) async-start(), calls=%async_computation.6 | async-start | bytes 524288 | tf_op jit(solution)/shard_map/psum | solution.py:189
  356.0 0.8 copy-start.9
Sparse Core Ops, SparseCore 0:
  218.2 136.7 all-reduce.6
where the time goes:
time: 365 us; the launch traced here: 364 us
  waiting for transfers between devices  168 us (46%)
  blocking collectives  92.2 us (25%)
  starting transfers between devices  41.2 us (11%)
  matrix products  28.5 us (8%)
  between operations  14.5 us (4%)
  local copies, waits for them, and re-layouts  13.5 us (4%)
  other arithmetic  6.89 us (2%)
    psum x1, waiting for transfers between devices, shards(): lax.psum((local_w_in, local_w_out, small_full), ('dp', 'seq'))  136 us
    psum x1, blocking collectives, shards(): lax.psum((local_w_in, local_w_out, small_full), ('dp', 'seq'))  67 us
    psum x1, blocking collectives, shards(): fg_blocks = lax.psum(fg_blocks, 'dp')  25.2 us
    all_to_all x1, starting transfers between devices, shards(): dp_blocks = lax.all_to_all(dp_blocks, 'seq', 2, 2, tiled=True)  14.6 us
    all_to_all x1, waiting for transfers between devices, shards(): lax.all_to_all(proj_blk.reshape(3, seq_n, per, block), 'seq', 1, 1, tiled...  13.9 us
    all_to_all x1, starting transfers between devices, shards(): rows_got = lax.all_to_all(rows_sent, 'seq', 0, 0, tiled=True)  9.43 us
    unnamed x37, local copies, waits for them, and re-layouts  8.79 us
    dot_general x5, matrix products, spectrum(): return jnp.einsum('kcm,mj->kcj', cat, tab['fwd2'], precision=HIGHEST)  8.23 us
  transfers between devices with their start and end apart: 7, of which 5 were waited for; matrix products, arithmetic and copies ran while one was open for 3% of the time, Pallas kernels for 0%

commit v1 on v0

--- a/solution.py
+++ b/solution.py
@@ -187,7 +187,7 @@
     small_full = jnp.zeros((3, 4, seq_n, per), jnp.float32)
     small_full = lax.dynamic_update_slice(small_full, small, (0, 0, me, 0))
     grad_w_in, grad_w_out, small_full = lax.psum(
-        (local_w_in, local_w_out, small_full), ("dp", "seq")
+        lax.psum((local_w_in, local_w_out, small_full), "dp"), "seq"
     )
     fg_blocks = lax.psum(fg_blocks, "dp")
     small_full = small_full.reshape(3, 4, width)

time: 365 us -> 406 us (1.11)
  waiting for transfers between devices: 168 us -> 242 us
  blocking collectives: 92.2 us -> 69.2 us
  starting transfers between devices: 41.2 us -> 31.1 us
    psum x1 -> x2, waiting for transfers between devices: 136 us -> 205 us  [the longest x1 144 us: shards(): lax.psum(lax.psum((local_w_in, local_w_out, small_full), 'dp'), 'seq')]
    psum x2, blocking collectives: 92.2 us -> 69.2 us  [the longest x1 41.2 us: shards(): lax.psum(lax.psum((local_w_in, local_w_out, small_full), 'dp'), 'seq')]
    all_to_all x1, starting transfers between devices: 14.6 us -> 5.08 us  [shards(): dp_blocks = lax.all_to_all(dp_blocks, 'seq', 2, 2, tiled=True)]
    all_to_all x1, waiting for transfers between devices: 0.01 us -> 4.39 us  [shards(): lax.all_to_all(filt_grad.reshape(2, seq_n, block), 'seq', 1, 1, tiled=True)]
  transfers between devices with their start and end apart: 7 -> 8, of which waited for: 5 -> 7; matrix products, arithmetic and copies ran while one was open for 3% -> 3% of each run, Pallas kernels for 0% -> 0%
where the time goes in v1:
time: 406 us; the launch traced here: 405 us
  waiting for transfers between devices  242 us (60%)
  blocking collectives  69.2 us (17%)
  starting transfers between devices  31.1 us (8%)
  matrix products  28.5 us (7%)
  between operations  14.6 us (4%)
  local copies, waits for them, and re-layouts  13.5 us (3%)
  other arithmetic  6.89 us (2%)
    psum x1, waiting for transfers between devices, shards(): lax.psum(lax.psum((local_w_in, local_w_out, small_full), 'dp'), 'seq')  144 us
    psum x1, waiting for transfers between devices, shards(): lax.psum((local_w_in, local_w_out, small_full), 'dp')  60.9 us
    psum x1, blocking collectives, shards(): lax.psum(lax.psum((local_w_in, local_w_out, small_full), 'dp'), 'seq')  41.2 us
    psum x1, blocking collectives, shards(): lax.psum((local_w_in, local_w_out, small_full), 'dp')  28.1 us
    all_to_all x1, waiting for transfers between devices, shards(): lax.all_to_all(proj_blk.reshape(3, seq_n, per, block), 'seq', 1, 1, tiled...  13.9 us
    all_to_all x1, starting transfers between devices, shards(): rows_got = lax.all_to_all(rows_sent, 'seq', 0, 0, tiled=True)  9.43 us
    all_to_all x1, waiting for transfers between devices, shards(): dp_blocks = lax.all_to_all(dp_blocks, 'seq', 2, 2, tiled=True)  8.91 us
    unnamed x37, local copies, waits for them, and re-layouts  8.79 us
  transfers between devices with their start and end apart: 8, of which 7 were waited for; matrix products, arithmetic and copies ran while one was open for 3% of the time, Pallas kernels for 0%

profile of v1, /device:TPU:1, one launch (start us, length us, event | category | flops | bytes accessed | tf_op | source)
XLA Modules:
  0.0 405.4 jit_solution(9546061533142303671)
XLA Ops:
  8.6 9.4 %all-to-all-start.1 = ((f32[16,2,512]{2,1,0:T(2,128)}), f32[16,2,512]{2,1,0:T(2,128)S(1)}, u32[]{:S(2)}, u32[]{:S(2)}) async-start(f32[16,2,512]{2,1,0:T(2,128)} %bitcast.12), calls=%async_computation.1 | async-start | bytes 131072 | tf_op jit(solution)/shard_map/all_to_all | solution.py:88
  20.6 1.2 fusion.68
  22.7 2.7 all-to-all-done.1
  25.4 4.6 %all-to-all-start.3 = ((f32[16,8,512]{2,1,0:T(8,128)}), f32[16,8,512]{2,1,0:T(8,128)S(1)}, u32[]{:S(2)}, u32[]{:S(2)}) async-start(f32[16,8,512]{2,1,0:T(8,128)} %fusion.70), calls=%async_computation.3 | async-start | bytes 524288 | tf_op jit(solution)/shard_map/all_to_all | solution.py:117
  31.8 6.9 %all-to-all-done.3 = f32[16,8,512]{2,1,0:T(8,128)S(1)} async-done(((f32[16,8,512]{2,1,0:T(8,128)}), f32[16,8,512]{2,1,0:T(8,128)S(1)}, u32[]{:S(2)}, u32[]{:S(2)}) %all-to-all-start.3) | async-done | bytes 262176 | tf_op jit(solution)/shard_map/all_to_all | solution.py:117
  38.7 4.2 %all-to-all-start = ((f32[3,16,8,512]{3,2,0,1:T(8,128)}), f32[3,16,8,512]{3,2,0,1:T(8,128)S(1)}, u32[]{:S(2)}, u32[]{:S(2)}) async-start(f32[3,16,8,512]{3,2,0,1:T(8,128)} %fusion.68), calls=%async_computation | async-start | bytes 1572864 | tf_op jit(solution)/shard_map/all_to_all | solution.py:98
  43.6 13.9 %all-to-all-done = f32[3,16,8,512]{3,2,0,1:T(8,128)S(1)} async-done(((f32[3,16,8,512]{3,2,0,1:T(8,128)}), f32[3,16,8,512]{3,2,0,1:T(8,128)S(1)}, u32[]{:S(2)}, u32[]{:S(2)}) %all-to-all-start) | async-done | bytes 786464 | tf_op jit(solution)/shard_map/all_to_all | solution.py:98
  59.1 1.0 fusion.64
  60.2 1.0 fusion.102
  61.3 1.9 fusion.25
  64.1 1.1 fusion.29
  66.1 1.1 convolution_add_fusion.1
  67.3 1.0 fusion.101
  68.5 1.9 fusion.3
  70.4 2.0 fusion.36
  72.9 1.1 fusion.7
  74.0 1.1 fusion.40
  75.4 1.1 convolution_add_fusion.3
  76.5 1.0 fusion.100
  77.7 1.9 fusion.14
  79.8 1.1 fusion.18
  81.1 1.1 convolution_add_fusion
  82.2 1.2 multiply_reduce_fusion.3
  86.7 4.0 all-to-all-start.5
  93.7 4.4 %all-to-all-done.5 = f32[2,16,512]{2,0,1:T(2,128)S(1)} async-done(((f32[2,16,512]{2,0,1:T(2,128)}), f32[2,16,512]{2,0,1:T(2,128)S(1)}, u32[]{:S(2)}, u32[]{:S(2)}) %all-to-all-start.5) | async-done | bytes 65568 | tf_op jit(solution)/shard_map/all_to_all | solution.py:170
  98.1 3.7 all-to-all-start.2
  101.8 28.1 %all-reduce.5 = (f32[3,4,16,8]{3,2,1,0:T(8,128)S(1)}, f32[2,8,512]{2,0,1:T(2,128)S(1)}) all-reduce(f32[3,4,16,8]{3,2,1,0:T(8,128)S(1)} %dynamic_update_slice.3, f32[2,8,512]{2,0,1:T(2,128)S(1)} %bitcast_reduce_fusion), channel_id=1, replica_groups=mesh['dp'=8,'seq'=16] {'dp'}, use_global_device_ids=true, to_apply=%region_9.10 | all-reduce | flops 9728 | bytes 77824 | tf_op jit(solution)/shard_map/psum | solution.py:190
  130.0 41.2 %psum.54 = f32[3,4,128]{2,1,0:T(4,128)S(1)} all-reduce(f32[3,4,128]{2,1,0:T(4,128)S(1)} %reshape.136), channel_id=1, replica_groups=mesh['dp'=8,'seq'=16] {'seq'}, use_global_device_ids=true, to_apply=%region_10.11 | all-reduce | flops 1536 | bytes 12288 | tf_op jit(solution)/shard_map/psum | solution.py:189
  171.2 5.1 %all-to-all-start.4 = ((bf16[3,8,16,512]{3,1,0,2:T(8,128)(2,1)}), bf16[3,8,16,512]{3,1,0,2:T(8,128)(2,1)S(1)}, u32[]{:S(2)}, u32[]{:S(2)}) async-start(bf16[3,8,16,512]{3,1,0,2:T(8,128)(2,1)} %copy.188), calls=%async_computation.4 | async-start | bytes 786432 | tf_op jit(solution)/shard_map/all_to_all | solution.py:162
  177.2 8.9 %all-to-all-done.4 = bf16[3,8,16,512]{3,1,0,2:T(8,128)(2,1)S(1)} async-done(((bf16[3,8,16,512]{3,1,0,2:T(8,128)(2,1)}), bf16[3,8,16,512]{3,1,0,2:T(8,128)(2,1)S(1)}, u32[]{:S(2)}, u32[]{:S(2)}) %all-to-all-start.4) | async-done | bytes 393248 | tf_op jit(solution)/shard_map/all_to_all | solution.py:162
  190.4 60.9 %all-reduce.12.cloned.1.call-done = (f32[128,384]{0,1:T(8,128)}, f32[128,128]{1,0:T(8,128)}) async-done(((f32[128,384]{0,1:T(8,128)}, f32[128,128]{1,0:T(8,128)}), (f32[128,384]{0,1:T(8,128)}, f32[128,128]{1,0:T(8,128)})) %all-reduce.12.cloned.1.call-update) | async-done | bytes 262160 | tf_op jit(solution)/shard_map/psum | solution.py:190
  252.2 143.9 %all-reduce.10.cloned.1.call-done = (f32[128,384]{0,1:T(8,128)}, f32[128,128]{1,0:T(8,128)}) async-done(((f32[128,384]{0,1:T(8,128)}, f32[128,128]{1,0:T(8,128)}), (f32[128,384]{0,1:T(8,128)}, f32[128,128]{1,0:T(8,128)})) %all-reduce.10.cloned.1.call-update) | async-done | bytes 262160 | tf_op jit(solution)/shard_map/psum | solution.py:189
  (108 shorter events, 27.0 us)
Async XLA Ops:
  7.2 13.4 %copy-start = (bf16[1,512,128]{2,1,0:T(8,128)(2,1)S(1)}, bf16[1,512,128]{2,1,0:T(8,128)(2,1)}, u32[]{:S(2)}) copy-start(bf16[1,512,128]{2,1,0:T(8,128)(2,1)} %param.15) | copy-start | bytes 393220
  8.6 10.5 %copy-start.8 = (bf16[128,384]{1,0:T(8,128)(2,1)S(1)}, bf16[128,384]{1,0:T(8,128)(2,1)}, u32[]{:S(2)}) copy-start(bf16[128,384]{1,0:T(8,128)(2,1)} %param.17) | copy-start | bytes 294916
  8.6 16.8 %all-to-all-start.1 = ((f32[16,2,512]{2,1,0:T(2,128)}), f32[16,2,512]{2,1,0:T(2,128)S(1)}, u32[]{:S(2)}, u32[]{:S(2)}) async-start(f32[16,2,512]{2,1,0:T(2,128)} %bitcast.12), calls=%async_computation.1 | async-start | bytes 131072 | tf_op jit(solution)/shard_map/all_to_all | solution.py:88
  18.1 0.7 copy-start.11
  19.2 0.7 copy-start.12
  19.8 0.7 copy-start.13
  20.6 1.2 copy-start.7
  20.6 1.2 copy-start.10
  25.4 13.3 %all-to-all-start.3 = ((f32[16,8,512]{2,1,0:T(8,128)}), f32[16,8,512]{2,1,0:T(8,128)S(1)}, u32[]{:S(2)}, u32[]{:S(2)}) async-start(f32[16,8,512]{2,1,0:T(8,128)} %fusion.70), calls=%async_computation.3 | async-start | bytes 524288 | tf_op jit(solution)/shard_map/all_to_all | solution.py:117
  30.0 0.8 copy-start.6
  30.8 0.8 copy-start.3
  30.8 0.9 copy-start.4
  31.8 11.1 %copy-start.2 = (f32[256,256,1]{1,0,2:T(8,128)S(1)}, f32[256,256,1]{1,0,2:T(8,128)}, u32[]{:S(2)}) copy-start(f32[256,256,1]{1,0,2:T(8,128)} %constant.59) | copy-start | bytes 786436
  38.7 18.8 %all-to-all-start = ((f32[3,16,8,512]{3,2,0,1:T(8,128)}), f32[3,16,8,512]{3,2,0,1:T(8,128)S(1)}, u32[]{:S(2)}, u32[]{:S(2)}) async-start(f32[3,16,8,512]{3,2,0,1:T(8,128)} %fusion.68), calls=%async_computation | async-start | bytes 1572864 | tf_op jit(solution)/shard_map/all_to_all | solution.py:98
  63.2 1.0 copy-start.1
  65.3 0.8 copy-start.5
  86.7 11.4 %all-to-all-start.5 = ((f32[2,16,512]{2,0,1:T(2,128)}), f32[2,16,512]{2,0,1:T(2,128)S(1)}, u32[]{:S(2)}, u32[]{:S(2)}) async-start(f32[2,16,512]{2,0,1:T(2,128)} %copy.198), calls=%async_computation.5 | async-start | bytes 131072 | tf_op jit(solution)/shard_map/all_to_all | solution.py:170
  98.1 73.1 %all-to-all-start.2 = ((bf16[16,4,8,128]{3,2,1,0:T(8,128)(2,1)}), bf16[16,4,8,128]{3,2,1,0:T(8,128)(2,1)S(1)}, u32[]{:S(2)}, u32[]{:S(2)}) async-start(bf16[16,4,8,128]{3,2,1,0:T(8,128)(2,1)} %copy.177), calls=%async_computation.2 | async-start | bytes 262144 | tf_op jit(solution)/shard_map/all_to_all | solution.py:153
  171.2 14.9 %all-to-all-start.4 = ((bf16[3,8,16,512]{3,1,0,2:T(8,128)(2,1)}), bf16[3,8,16,512]{3,1,0,2:T(8,128)(2,1)S(1)}, u32[]{:S(2)}, u32[]{:S(2)}) async-start(bf16[3,8,16,512]{3,1,0,2:T(8,128)(2,1)} %copy.188), calls=%async_computation.4 | async-start | bytes 786432 | tf_op jit(solution)/shard_map/all_to_all | solution.py:162
  176.3 74.9 %all-reduce.12.cloned.1.call-start = ((), (), s32[]{:S(2)}) async-start(), calls=%async_computation.7 | async-start | bytes 524288 | tf_op jit(solution)/shard_map/psum | solution.py:190
  187.1 209.0 %all-reduce.10.cloned.1.call-start = ((), (), s32[]{:S(2)}) async-start(), calls=%async_computation.6 | async-start | bytes 524288 | tf_op jit(solution)/shard_map/psum | solution.py:189
  397.0 0.8 copy-start.9
Sparse Core Ops, SparseCore 0:
  187.2 63.9 all-reduce.11
  253.9 142.1 all-reduce.9
